TPU v7x, 32 devices: a whole 2x2x4 slice. The times are simulated.
32 devices in a mesh: seq: 8 (over z, x), head: 2 (over y), dp: 2 (over core).
Axes of the slice: x: 2, y: 2, z: 4, core: 2. Of those that a mesh axis runs over, the one named last changes fastest.
Arguments:
- queries: bfloat16 [2, 2048, 1024], P('dp', 'seq', 'head'), may hold values from -6 to 6
- key_rows: bfloat16 [2, 2048, 1024], P('dp', 'seq', 'head'), may hold values from -6 to 6
- value_rows: bfloat16 [2, 2048, 1024], P('dp', 'seq', 'head'), may hold values from -140 to 140
- stretch_doc: int32 [2, 8], P('dp', 'seq'), may hold values from 0 to 3, never falling along the last dimension, each value on 1 to 4 neighbouring positions
- head_gain: float32 [8, 128], P('head'), may hold values from 0.1 to 1.9
- w_out: bfloat16 [1024, 2048], P('head'), may hold values from -0.1875 to 0.1875
- cotangent: bfloat16 [2, 2048, 2048], P('dp', 'seq'), may hold values from -40 to 40
Outputs:
- layer_out: bfloat16 [2, 2048, 2048], P('dp', ('seq', 'head'))
- query_grad: bfloat16 [2, 2048, 1024], P('dp', 'seq', 'head')
- key_grad: bfloat16 [2, 2048, 1024], P('dp', 'seq', 'head')
- value_grad: bfloat16 [2, 2048, 1024], P('dp', 'seq', 'head')
- gain_grad: float32 [8, 128], P('head')
Inputs may be any that keep to these rules, and one draw needn't show every extreme that they name: `stretch_doc`: document numbers never fall along a sequence; each document spans 1 to 4 whole stretches, and one spans exactly that many.
All inputs are finite; a program needn't handle non-finite values.
Results may differ from a plain program's by a relative error of at most 0.0055.
Values may be sent and summed in bfloat16 or wider, within the bound.
No kernel may reach another device: no remote copies, remote signals or barrier semaphores. Data moves between devices by JAX's collectives and lax.ppermute only.
A program may use at most 64 MiB of HBM per device.

v0:
```python
import math
import jax
import jax.numpy as jnp
from jax import lax
from jax.sharding import PartitionSpec as P

epsilon = 1e-05
highest = lax.Precision.HIGHEST


def shifted(block, axis, distance):
    devices = range(lax.axis_size(axis))
    route = [(i - distance, i) for i in devices if i - distance in devices]
    return lax.ppermute(block, axis, route)


def link_docs(earlier, following):
    sum_early, doc_early = earlier
    sum_late, doc_late = following
    merged = jnp.where(doc_early[0] == doc_late[0], sum_late + sum_early, sum_late)
    running = jnp.where(doc_late[0] < 0.5, sum_early, merged)
    return (running, jnp.where(doc_late < 0.5, doc_early, doc_late))


def double_chain(start, mover, seq_size):
    current = mover(start, 1)
    reach = 1
    while reach < seq_size - 1:
        current = link_docs(mover(current, reach), current)
        reach = reach * 2
    return current


def on_device(queries, key_rows, value_rows, stretch_doc, head_gain, w_out, cotangent):
    token_count = queries.shape[1]
    local_width = queries.shape[2]
    head_count = head_gain.shape[0]
    head_dim = head_gain.shape[1]
    stretches = stretch_doc.shape[1]
    stretch_len = token_count // stretches
    seq_size = lax.axis_size("seq")
    blocks = (stretches, stretch_len, head_count, head_dim)
    query_blk = queries[0].reshape(blocks)
    key_blk = key_rows[0].reshape(blocks)
    value_blk = value_rows[0].reshape(blocks)
    doc_ids = stretch_doc[0]
    doc_float = doc_ids.astype(jnp.float32) + 1.0
    stretch_order = jnp.arange(stretches)
    same_doc = doc_ids[:, None] == doc_ids[None, :]
    before_mask = jnp.where(
        same_doc & (stretch_order[None, :] < stretch_order[:, None]), 1.0, 0.0
    ).astype(jnp.float32)
    after_mask = jnp.where(
        same_doc & (stretch_order[None, :] > stretch_order[:, None]), 1.0, 0.0
    ).astype(jnp.float32)
    positions = jnp.arange(stretch_len)
    causal = positions[:, None] >= positions[None, :]

    def move_forward(pair, distance):
        return shifted((pair[0], pair[1]), "seq", distance)

    def move_backward(pair, distance):
        return shifted((pair[0], pair[1]), "seq", -distance)

    kv_sum = jnp.einsum("cshd,cshe->chde", key_blk, value_blk, preferred_element_type=jnp.float32)
    last_pick = jnp.where(doc_float == doc_float[0], 1.0, 0.0).astype(jnp.float32)
    own_state = jnp.einsum("c,chde->hde", last_pick, kv_sum, precision=highest)
    incoming, incoming_doc = double_chain((own_state, doc_float), move_forward, seq_size)
    take_in = jnp.where(doc_float == incoming_doc[0], 1.0, 0.0).astype(jnp.float32)
    states = (
        jnp.einsum("cj,jhde->chde", before_mask, kv_sum, precision=highest)
        + take_in[:, None, None, None] * incoming
    )
    scores = jnp.einsum("cthd,cshd->chts", query_blk, key_blk, preferred_element_type=jnp.float32)
    attn_weights = jnp.where(causal, scores, 0.0).astype(jnp.bfloat16)
    within = jnp.einsum(
        "chts,cshe->cthe", attn_weights, value_blk, preferred_element_type=jnp.float32
    )
    query_f = query_blk.astype(jnp.float32)
    carried = jnp.einsum("cthd,chde->cthe", query_f, states, precision=highest)
    attended = within + carried
    inv_rms = lax.rsqrt(jnp.mean(attended * attended, axis=-1, keepdims=True) + epsilon)
    unit_rows = attended * inv_rms
    normed_rows = (unit_rows * head_gain).astype(jnp.bfloat16).reshape(token_count, local_width)
    exchanged = lax.all_to_all(normed_rows, "head", split_axis=0, concat_axis=1, tiled=True)
    summed = jnp.dot(
        exchanged,
        lax.all_gather(w_out, "head", axis=0, tiled=True),
        preferred_element_type=jnp.float32,
    )
    layer_out = summed.astype(jnp.bfloat16)[None]
    grad_normed = jnp.einsum(
        "tm,fm->tf", cotangent[0], w_out, preferred_element_type=jnp.float32
    ).reshape(blocks)
    gain_part = jnp.sum(grad_normed * unit_rows, axis=(0, 1))
    total_tokens = seq_size * lax.axis_size("dp") * token_count
    gain_grad = lax.psum(gain_part, ("seq", "dp")) / math.sqrt(total_tokens)
    scaled = grad_normed * head_gain
    grad_attended = inv_rms * (
        scaled - unit_rows * jnp.mean(scaled * unit_rows, axis=-1, keepdims=True)
    )
    grad_bf = grad_attended.astype(jnp.bfloat16)
    query_term = jnp.einsum(
        "cthd,cthe->chde", query_blk, grad_bf, preferred_element_type=jnp.float32
    )
    first_pick = jnp.where(doc_float == doc_float[0], 1.0, 0.0).astype(jnp.float32)
    own_grad = jnp.einsum("c,chde->hde", first_pick, query_term, precision=highest)
    incoming_grad, grad_doc = double_chain((own_grad, doc_float), move_backward, seq_size)
    take_back = jnp.where(doc_float == grad_doc[0], 1.0, 0.0).astype(jnp.float32)
    grad_states = (
        jnp.einsum("cj,jhde->chde", after_mask, query_term, precision=highest)
        + take_back[:, None, None, None] * incoming_grad
    )
    grad_scores = jnp.einsum(
        "cthe,cshe->chts", grad_bf, value_blk, preferred_element_type=jnp.float32
    )
    grad_weights = jnp.where(causal, grad_scores, 0.0).astype(jnp.bfloat16)
    grad_f = grad_bf.astype(jnp.float32)
    query_grad = jnp.einsum(
        "chts,cshd->cthd", grad_weights, key_blk, preferred_element_type=jnp.float32
    ) + jnp.einsum("cthe,chde->cthd", grad_f, states, precision=highest)
    key_grad = jnp.einsum(
        "chts,cthd->cshd", grad_weights, query_blk, preferred_element_type=jnp.float32
    ) + jnp.einsum("cshe,chde->cshd", value_blk.astype(jnp.float32), grad_states, precision=highest)
    value_grad = jnp.einsum(
        "chts,cthe->cshe", attn_weights, grad_bf, preferred_element_type=jnp.float32
    ) + jnp.einsum("cshd,chde->cshe", key_blk.astype(jnp.float32), grad_states, precision=highest)
    out_shape = (1, token_count, local_width)
    return (
        layer_out,
        query_grad.astype(jnp.bfloat16).reshape(out_shape),
        key_grad.astype(jnp.bfloat16).reshape(out_shape),
        value_grad.astype(jnp.bfloat16).reshape(out_shape),
        gain_grad,
    )


def solution(mesh):
    return jax.shard_map(
        on_device,
        mesh=mesh,
        in_specs=(
            P("dp", "seq", "head"),
            P("dp", "seq", "head"),
            P("dp", "seq", "head"),
            P("dp", "seq"),
            P("head", None),
            P("head", None),
            P("dp", "seq", None),
        ),
        out_specs=(
            P("dp", ("seq", "head"), None),
            P("dp", "seq", "head"),
            P("dp", "seq", "head"),
            P("dp", "seq", "head"),
            P("head", None),
        ),
        check_vma=False,
    )
```

profile of v0, /device:TPU:7, one launch (start us, length us, event | category | flops | bytes accessed | tf_op | source)
XLA Modules:
  0.0 170.7 jit_solution(11719621536188737796)
XLA Ops:
  8.0 1.0 reshape.195
  9.2 1.0 reshape.196
  10.5 3.2 %collective-permute-start.4 = (f32[4,128,128]{2,1,0:T(8,128)S(1)}, f32[4,128,128]{2,1,0:T(8,128)S(1)}, u32[]{:S(2)}, u32[]{:S(2)}) collective-permute-start(f32[4,128,128]{2,1,0:T(8,128)S(1)} %get-tuple-element.19), channel_id=1, source_target_pairs={{0,4},{4,8},{8,12},{12,16},{16,20},{20,24},{24,28},{1,5},{5,9},{9,... | collective-permute-start | bytes 786440 | tf_op jit(solution)/shard_map/ppermute | solution.py:14
  13.6 5.9 %collective-permute-done.4 = f32[4,128,128]{2,1,0:T(8,128)S(1)} collective-permute-done((f32[4,128,128]{2,1,0:T(8,128)S(1)}, f32[4,128,128]{2,1,0:T(8,128)S(1)}, u32[]{:S(2)}, u32[]{:S(2)}) %collective-permute-start.4) | collective-permute-done | bytes 262176 | tf_op jit(solution)/shard_map/ppermute | solution.py:14
  19.5 4.0 %collective-permute-start.5 = (f32[4,128,128]{2,1,0:T(8,128)S(1)}, f32[4,128,128]{2,1,0:T(8,128)S(1)}, u32[]{:S(2)}, u32[]{:S(2)}) collective-permute-start(f32[4,128,128]{2,1,0:T(8,128)S(1)} %collective-permute-done.4), channel_id=1, source_target_pairs={{0,4},{4,8},{8,12},{12,16},{16,20},{20,24},{24,28},{1,5},{5,9},{9,... | collective-permute-start | bytes 786440 | tf_op jit(solution)/shard_map/ppermute | solution.py:14
  23.6 4.1 %collective-permute-start = (f32[1]{0:T(128)}, f32[1]{0:T(128)}, u32[]{:S(2)}, u32[]{:S(2)}) collective-permute-start(f32[1]{0:T(128)} %bitcast.1), channel_id=1, source_target_pairs={{0,4},{4,8},{8,12},{12,16},{16,20},{20,24},{24,28},{1,5},{5,9},{9,... | collective-permute-start | bytes 20 | tf_op jit(solution)/shard_map/ppermute | solution.py:14
  28.2 4.4 %collective-permute-start.1 = (f32[1]{0:T(128)}, f32[1]{0:T(128)}, u32[]{:S(2)}, u32[]{:S(2)}) collective-permute-start(f32[1]{0:T(128)} %collective-permute-done), channel_id=1, source_target_pairs={{0,4},{4,8},{8,12},{12,16},{16,20},{20,24},{24,28},{1,5},{5,9},{9,... | collective-permute-start | bytes 20 | tf_op jit(solution)/shard_map/ppermute | solution.py:14
  34.8 3.2 %collective-permute-start.6 = (f32[4,128,128]{2,1,0:T(8,128)S(1)}, f32[4,128,128]{2,1,0:T(8,128)S(1)}, u32[]{:S(2)}, u32[]{:S(2)}) collective-permute-start(f32[4,128,128]{2,1,0:T(8,128)S(1)} %fusion.14), channel_id=1, source_target_pairs={{0,8},{4,12},{8,16},{12,20},{16,24},{20,28},{1,9},{5,13},{9,17},{1... | collective-permute-start | bytes 786440 | tf_op jit(solution)/shard_map/ppermute | solution.py:14
  38.1 2.7 %fusion.7 = f32[256,512]{0,1:T(8,128)S(1)} fusion(bf16[512,2048]{1,0:T(8,128)(2,1)} %param.12, bf16[1,256,2048]{2,1,0:T(8,128)(2,1)S(1)} %copy-done), kind=kOutput, calls=%fused_computation.17 | convolution fusion | flops 536870912 | bytes 3670016 | tf_op jit(solution)/shard_map/tm,fm->tf/dot_general | solution.py:92
  42.0 3.9 %collective-permute-start.2 = (f32[1]{0:T(128)}, f32[1]{0:T(128)}, u32[]{:S(2)}, u32[]{:S(2)}) collective-permute-start(f32[1]{0:T(128)} %select_n.117), channel_id=1, source_target_pairs={{0,8},{4,12},{8,16},{12,20},{16,24},{20,28},{1,9},{5,13},{9,17},{1... | collective-permute-start | bytes 20 | tf_op jit(solution)/shard_map/ppermute | solution.py:14
  46.6 4.2 %collective-permute-start.7 = (f32[4,128,128]{2,1,0:T(8,128)S(1)}, f32[4,128,128]{2,1,0:T(8,128)S(1)}, u32[]{:S(2)}, u32[]{:S(2)}) collective-permute-start(f32[4,128,128]{2,1,0:T(8,128)S(1)} %fusion.13), channel_id=1, source_target_pairs={{0,16},{4,20},{8,24},{12,28},{1,17},{5,21},{9,25},{13,29},{2,18},{... | collective-permute-start | bytes 786440 | tf_op jit(solution)/shard_map/ppermute | solution.py:14
  52.1 2.1 %collective-permute-start.3 = (f32[1]{0:T(128)}, f32[1]{0:T(128)}, u32[]{:S(2)}, u32[]{:S(2)}) collective-permute-start(f32[1]{0:T(128)} %select_n.118), channel_id=1, source_target_pairs={{0,16},{4,20},{8,24},{12,28},{1,17},{5,21},{9,25},{13,29},{2,18},{... | collective-permute-start | bytes 20 | tf_op jit(solution)/shard_map/ppermute | solution.py:14
  57.4 4.2 %collective-permute-start.12 = (f32[4,128,128]{1,2,0:T(8,128)S(1)}, f32[4,128,128]{1,2,0:T(8,128)S(1)}, u32[]{:S(2)}, u32[]{:S(2)}) collective-permute-start(f32[4,128,128]{1,2,0:T(8,128)S(1)} %multiply_bitcast_fusion), channel_id=1, source_target_pairs={{4,0},{8,4},{12,8},{16,12},{20,16},{24,20},{28,24},{5,1},{9,5},{13... | collective-permute-start | bytes 786440 | tf_op jit(solution)/shard_map/ppermute | solution.py:14
  61.5 3.3 %collective-permute-start.8 = (f32[1]{0:T(128)}, f32[1]{0:T(128)}, u32[]{:S(2)}, u32[]{:S(2)}) collective-permute-start(f32[1]{0:T(128)} %bitcast.1), channel_id=1, source_target_pairs={{4,0},{8,4},{12,8},{16,12},{20,16},{24,20},{28,24},{5,1},{9,5},{13... | collective-permute-start | bytes 20 | tf_op jit(solution)/shard_map/ppermute | solution.py:14
  64.9 7.3 %collective-permute-done.8 = f32[1]{0:T(128)} collective-permute-done((f32[1]{0:T(128)}, f32[1]{0:T(128)}, u32[]{:S(2)}, u32[]{:S(2)}) %collective-permute-start.8) | collective-permute-done | bytes 36 | tf_op jit(solution)/shard_map/ppermute | solution.py:14
  72.1 1.9 %collective-permute-start.9 = (f32[1]{0:T(128)}, f32[1]{0:T(128)}, u32[]{:S(2)}, u32[]{:S(2)}) collective-permute-start(f32[1]{0:T(128)} %collective-permute-done.8), channel_id=1, source_target_pairs={{4,0},{8,4},{12,8},{16,12},{20,16},{24,20},{28,24},{5,1},{9,5},{13... | collective-permute-start | bytes 20 | tf_op jit(solution)/shard_map/ppermute | solution.py:14
  74.6 2.8 %collective-permute-done.9 = f32[1]{0:T(128)} collective-permute-done((f32[1]{0:T(128)}, f32[1]{0:T(128)}, u32[]{:S(2)}, u32[]{:S(2)}) %collective-permute-start.9) | collective-permute-done | bytes 36 | tf_op jit(solution)/shard_map/ppermute | solution.py:14
  78.7 1.3 collective-permute-start.10
  81.2 2.3 %collective-permute-done.10 = f32[1]{0:T(128)} collective-permute-done((f32[1]{0:T(128)}, f32[1]{0:T(128)}, u32[]{:S(2)}, u32[]{:S(2)}) %collective-permute-start.10) | collective-permute-done | bytes 36 | tf_op jit(solution)/shard_map/ppermute | solution.py:14
  84.1 1.3 collective-permute-start.11
  86.1 3.4 %collective-permute-done.11 = f32[1]{0:T(128)} collective-permute-done((f32[1]{0:T(128)}, f32[1]{0:T(128)}, u32[]{:S(2)}, u32[]{:S(2)}) %collective-permute-start.11) | collective-permute-done | bytes 36 | tf_op jit(solution)/shard_map/ppermute | solution.py:14
  90.8 1.9 %collective-permute-start.13 = (f32[4,128,128]{1,2,0:T(8,128)S(1)}, f32[4,128,128]{1,2,0:T(8,128)S(1)}, u32[]{:S(2)}, u32[]{:S(2)}) collective-permute-start(f32[4,128,128]{1,2,0:T(8,128)S(1)} %collective-permute-done.12), channel_id=1, source_target_pairs={{4,0},{8,4},{12,8},{16,12},{20,16},{24,20},{28,24},{5,1},{9,5},{13... | collective-permute-start | bytes 786440 | tf_op jit(solution)/shard_map/ppermute | solution.py:14
  93.4 5.4 %collective-permute-done.13 = f32[4,128,128]{1,2,0:T(8,128)S(1)} collective-permute-done((f32[4,128,128]{1,2,0:T(8,128)S(1)}, f32[4,128,128]{1,2,0:T(8,128)S(1)}, u32[]{:S(2)}, u32[]{:S(2)}) %collective-permute-start.13) | collective-permute-done | bytes 262176 | tf_op jit(solution)/shard_map/ppermute | solution.py:14
  98.9 1.3 collective-permute-start.14
  101.4 1.0 all_to_all.14
  103.1 3.4 %all-to-all-start = ((bf16[2,128,512]{1,2,0:T(8,128)(2,1)}), bf16[2,128,512]{1,2,0:T(8,128)(2,1)S(1)}, u32[]{:S(2)}, u32[]{:S(2)}) async-start(bf16[2,128,512]{1,2,0:T(8,128)(2,1)} %copy.39), calls=%async_computation | async-start | bytes 524288 | tf_op jit(solution)/shard_map/all_to_all | solution.py:85
  106.6 33.1 %psum.7 = f32[4,128]{1,0:T(4,128)S(1)} all-reduce(f32[4,128]{1,0:T(4,128)S(1)} %get-tuple-element.15), channel_id=1, replica_groups=mesh['seq'=8,'head'=2,'dp'=2] {'seq','dp'}, use_global_device_ids=true, to_apply=%region_3.4 | all-reduce | flops 512 | bytes 4096 | tf_op jit(solution)/shard_map/psum | solution.py:97
  140.0 1.0 fusion.10
  140.9 1.3 collective-permute-start.15
  142.8 1.3 convolution_bitcast_fusion
  144.1 13.4 %collective-permute-done.15 = f32[4,128,128]{1,2,0:T(8,128)S(1)} collective-permute-done((f32[4,128,128]{1,2,0:T(8,128)S(1)}, f32[4,128,128]{1,2,0:T(8,128)S(1)}, u32[]{:S(2)}, u32[]{:S(2)}) %collective-permute-start.15) | collective-permute-done | bytes 262176 | tf_op jit(solution)/shard_map/ppermute | solution.py:14
  160.2 3.7 %fusion = bf16[1,128,2048]{2,1,0:T(8,128)(2,1)} fusion(bf16[128,1024]{0,1:T(8,128)(2,1)S(1)} %bitcast.79, bf16[1024,2048]{1,0:T(8,128)(2,1)} %all-gather.2.cloned.1.call-done), kind=kOutput, calls=%fused_computation.1 | convolution fusion | flops 537133056 | bytes 4980736 | tf_op jit(solution)/shard_map/dot_general | solution.py:86
  (50 shorter events, 9.8 us)
Async XLA Ops:
  7.2 30.9 %copy-start = (bf16[1,256,2048]{2,1,0:T(8,128)(2,1)S(1)}, bf16[1,256,2048]{2,1,0:T(8,128)(2,1)}, u32[]{:S(2)}) copy-start(bf16[1,256,2048]{2,1,0:T(8,128)(2,1)} %param.13) | copy-start | bytes 3145732
  7.2 20.5 %copy-start.2 = (bf16[1,256,512]{2,1,0:T(8,128)(2,1)S(1)}, bf16[1,256,512]{2,1,0:T(8,128)(2,1)}, u32[]{:S(2)}) copy-start(bf16[1,256,512]{2,1,0:T(8,128)(2,1)} %param.7) | copy-start | bytes 786436
  7.2 153.0 %all-gather.2.cloned.1.call-start = ((), (), s32[]{:S(2)}) async-start(), calls=%async_computation.1 | async-start | bytes 6291456 | tf_op jit(solution)/shard_map/all_gather | solution.py:88
  10.5 9.1 %collective-permute-start.4 = (f32[4,128,128]{2,1,0:T(8,128)S(1)}, f32[4,128,128]{2,1,0:T(8,128)S(1)}, u32[]{:S(2)}, u32[]{:S(2)}) collective-permute-start(f32[4,128,128]{2,1,0:T(8,128)S(1)} %get-tuple-element.19), channel_id=1, source_target_pairs={{0,4},{4,8},{8,12},{12,16},{16,20},{20,24},{24,28},{1,5},{5,9},{9,... | collective-permute-start | bytes 786440 | tf_op jit(solution)/shard_map/ppermute | solution.py:14
  19.5 15.3 %collective-permute-start.5 = (f32[4,128,128]{2,1,0:T(8,128)S(1)}, f32[4,128,128]{2,1,0:T(8,128)S(1)}, u32[]{:S(2)}, u32[]{:S(2)}) collective-permute-start(f32[4,128,128]{2,1,0:T(8,128)S(1)} %collective-permute-done.4), channel_id=1, source_target_pairs={{0,4},{4,8},{8,12},{12,16},{16,20},{20,24},{24,28},{1,5},{5,9},{9,... | collective-permute-start | bytes 786440 | tf_op jit(solution)/shard_map/ppermute | solution.py:14
  23.6 4.6 %collective-permute-start = (f32[1]{0:T(128)}, f32[1]{0:T(128)}, u32[]{:S(2)}, u32[]{:S(2)}) collective-permute-start(f32[1]{0:T(128)} %bitcast.1), channel_id=1, source_target_pairs={{0,4},{4,8},{8,12},{12,16},{16,20},{20,24},{24,28},{1,5},{5,9},{9,... | collective-permute-start | bytes 20 | tf_op jit(solution)/shard_map/ppermute | solution.py:14
  28.2 5.3 %collective-permute-start.1 = (f32[1]{0:T(128)}, f32[1]{0:T(128)}, u32[]{:S(2)}, u32[]{:S(2)}) collective-permute-start(f32[1]{0:T(128)} %collective-permute-done), channel_id=1, source_target_pairs={{0,4},{4,8},{8,12},{12,16},{16,20},{20,24},{24,28},{1,5},{5,9},{9,... | collective-permute-start | bytes 20 | tf_op jit(solution)/shard_map/ppermute | solution.py:14
  34.8 21.2 %copy-start.3 = (f32[4,128]{1,0:T(4,128)S(1)}, f32[4,128]{1,0:T(4,128)}, u32[]{:S(2)}) copy-start(f32[4,128]{1,0:T(4,128)} %param.11) | copy-start | bytes 6148
  34.8 11.7 %collective-permute-start.6 = (f32[4,128,128]{2,1,0:T(8,128)S(1)}, f32[4,128,128]{2,1,0:T(8,128)S(1)}, u32[]{:S(2)}, u32[]{:S(2)}) collective-permute-start(f32[4,128,128]{2,1,0:T(8,128)S(1)} %fusion.14), channel_id=1, source_target_pairs={{0,8},{4,12},{8,16},{12,20},{16,24},{20,28},{1,9},{5,13},{9,17},{1... | collective-permute-start | bytes 786440 | tf_op jit(solution)/shard_map/ppermute | solution.py:14
  42.0 3.9 %collective-permute-start.2 = (f32[1]{0:T(128)}, f32[1]{0:T(128)}, u32[]{:S(2)}, u32[]{:S(2)}) collective-permute-start(f32[1]{0:T(128)} %select_n.117), channel_id=1, source_target_pairs={{0,8},{4,12},{8,16},{12,20},{16,24},{20,28},{1,9},{5,13},{9,17},{1... | collective-permute-start | bytes 20 | tf_op jit(solution)/shard_map/ppermute | solution.py:14
  46.6 8.8 %collective-permute-start.7 = (f32[4,128,128]{2,1,0:T(8,128)S(1)}, f32[4,128,128]{2,1,0:T(8,128)S(1)}, u32[]{:S(2)}, u32[]{:S(2)}) collective-permute-start(f32[4,128,128]{2,1,0:T(8,128)S(1)} %fusion.13), channel_id=1, source_target_pairs={{0,16},{4,20},{8,24},{12,28},{1,17},{5,21},{9,25},{13,29},{2,18},{... | collective-permute-start | bytes 786440 | tf_op jit(solution)/shard_map/ppermute | solution.py:14
  52.1 2.1 %collective-permute-start.3 = (f32[1]{0:T(128)}, f32[1]{0:T(128)}, u32[]{:S(2)}, u32[]{:S(2)}) collective-permute-start(f32[1]{0:T(128)} %select_n.118), channel_id=1, source_target_pairs={{0,16},{4,20},{8,24},{12,28},{1,17},{5,21},{9,25},{13,29},{2,18},{... | collective-permute-start | bytes 20 | tf_op jit(solution)/shard_map/ppermute | solution.py:14
  57.4 33.4 %collective-permute-start.12 = (f32[4,128,128]{1,2,0:T(8,128)S(1)}, f32[4,128,128]{1,2,0:T(8,128)S(1)}, u32[]{:S(2)}, u32[]{:S(2)}) collective-permute-start(f32[4,128,128]{1,2,0:T(8,128)S(1)} %multiply_bitcast_fusion), channel_id=1, source_target_pairs={{4,0},{8,4},{12,8},{16,12},{20,16},{24,20},{28,24},{5,1},{9,5},{13... | collective-permute-start | bytes 786440 | tf_op jit(solution)/shard_map/ppermute | solution.py:14
  61.5 10.6 %collective-permute-start.8 = (f32[1]{0:T(128)}, f32[1]{0:T(128)}, u32[]{:S(2)}, u32[]{:S(2)}) collective-permute-start(f32[1]{0:T(128)} %bitcast.1), channel_id=1, source_target_pairs={{4,0},{8,4},{12,8},{16,12},{20,16},{24,20},{28,24},{5,1},{9,5},{13... | collective-permute-start | bytes 20 | tf_op jit(solution)/shard_map/ppermute | solution.py:14
  72.1 5.3 %collective-permute-start.9 = (f32[1]{0:T(128)}, f32[1]{0:T(128)}, u32[]{:S(2)}, u32[]{:S(2)}) collective-permute-start(f32[1]{0:T(128)} %collective-permute-done.8), channel_id=1, source_target_pairs={{4,0},{8,4},{12,8},{16,12},{20,16},{24,20},{28,24},{5,1},{9,5},{13... | collective-permute-start | bytes 20 | tf_op jit(solution)/shard_map/ppermute | solution.py:14
  78.7 4.8 %collective-permute-start.10 = (f32[1]{0:T(128)}, f32[1]{0:T(128)}, u32[]{:S(2)}, u32[]{:S(2)}) collective-permute-start(f32[1]{0:T(128)} %select_n.135), channel_id=1, source_target_pairs={{8,0},{12,4},{16,8},{20,12},{24,16},{28,20},{9,1},{13,5},{17,9},{2... | collective-permute-start | bytes 20 | tf_op jit(solution)/shard_map/ppermute | solution.py:14
  84.1 5.4 %collective-permute-start.11 = (f32[1]{0:T(128)}, f32[1]{0:T(128)}, u32[]{:S(2)}, u32[]{:S(2)}) collective-permute-start(f32[1]{0:T(128)} %select_n.136), channel_id=1, source_target_pairs={{16,0},{20,4},{24,8},{28,12},{17,1},{21,5},{25,9},{29,13},{18,2},{... | collective-permute-start | bytes 20 | tf_op jit(solution)/shard_map/ppermute | solution.py:14
  90.8 8.0 %collective-permute-start.13 = (f32[4,128,128]{1,2,0:T(8,128)S(1)}, f32[4,128,128]{1,2,0:T(8,128)S(1)}, u32[]{:S(2)}, u32[]{:S(2)}) collective-permute-start(f32[4,128,128]{1,2,0:T(8,128)S(1)} %collective-permute-done.12), channel_id=1, source_target_pairs={{4,0},{8,4},{12,8},{16,12},{20,16},{24,20},{28,24},{5,1},{9,5},{13... | collective-permute-start | bytes 786440 | tf_op jit(solution)/shard_map/ppermute | solution.py:14
  93.1 7.4 %copy-start.1 = (bf16[4,256,256]{2,1,0:T(8,128)(2,1)}, bf16[4,256,256]{2,1,0:T(8,128)(2,1)S(1)}, u32[]{:S(2)}) copy-start(bf16[4,256,256]{2,1,0:T(8,128)(2,1)S(1)} %fusion.2) | copy-start | bytes 1572868
  98.9 41.1 %collective-permute-start.14 = (f32[4,128,128]{1,2,0:T(8,128)S(1)}, f32[4,128,128]{1,2,0:T(8,128)}, u32[]{:S(2)}, u32[]{:S(2)}) collective-permute-start(f32[4,128,128]{1,2,0:T(8,128)S(1)} %fusion.11), channel_id=1, source_target_pairs={{8,0},{12,4},{16,8},{20,12},{24,16},{28,20},{9,1},{13,5},{17,9},{2... | collective-permute-start | bytes 786440 | tf_op jit(solution)/shard_map/ppermute | solution.py:14
  103.1 57.0 %all-to-all-start = ((bf16[2,128,512]{1,2,0:T(8,128)(2,1)}), bf16[2,128,512]{1,2,0:T(8,128)(2,1)S(1)}, u32[]{:S(2)}, u32[]{:S(2)}) async-start(bf16[2,128,512]{1,2,0:T(8,128)(2,1)} %copy.39), calls=%async_computation | async-start | bytes 524288 | tf_op jit(solution)/shard_map/all_to_all | solution.py:85
  140.9 16.6 %collective-permute-start.15 = (f32[4,128,128]{1,2,0:T(8,128)S(1)}, f32[4,128,128]{1,2,0:T(8,128)S(1)}, u32[]{:S(2)}, u32[]{:S(2)}) collective-permute-start(f32[4,128,128]{1,2,0:T(8,128)S(1)} %fusion.10), channel_id=1, source_target_pairs={{16,0},{20,4},{24,8},{28,12},{17,1},{21,5},{25,9},{29,13},{18,2},{... | collective-permute-start | bytes 786440 | tf_op jit(solution)/shard_map/ppermute | solution.py:14
Sparse Core Ops, SparseCore 0:
  27.8 57.8 all-gather.1
where the time goes:
time: 172 us; the launch traced here: 171 us
  starting transfers between devices  49.1 us (29%)
  waiting for transfers between devices  41.2 us (24%)
  blocking collectives  33.1 us (19%)
  between operations  26.5 us (15%)
  matrix products  11.2 us (7%)
  local copies, waits for them, and re-layouts  6.59 us (4%)
  other arithmetic  2.95 us (2%)
    ppermute x16, starting transfers between devices, shifted(): return lax.ppermute(block, axis, route)  45.6 us
    ppermute x16, waiting for transfers between devices, shifted(): return lax.ppermute(block, axis, route)  41.2 us
    psum x1, blocking collectives, on_device(): gain_grad = lax.psum(gain_part, ('seq', 'dp')) / math.sqrt(total_tokens)  33.1 us
    dot_general x1, matrix products, on_device(): jnp.dot(exchanged, lax.all_gather(w_out, 'head', axis=0, tiled=True), pre...  3.72 us
  transfers between devices with their start and end apart: 18, of which 9 were waited for; matrix products, arithmetic and copies ran while one was open for 8% of the time, Pallas kernels for 0%

commit v1 on v0

--- a/solution.py
+++ b/solution.py
@@ -94,7 +94,7 @@
     ).reshape(blocks)
     gain_part = jnp.sum(grad_normed * unit_rows, axis=(0, 1))
     total_tokens = seq_size * lax.axis_size("dp") * token_count
-    gain_grad = lax.psum(gain_part, ("seq", "dp")) / math.sqrt(total_tokens)
+    gain_grad = jnp.sum(lax.all_gather(gain_part, ("seq", "dp")), axis=0) / math.sqrt(total_tokens)
     scaled = grad_normed * head_gain
     grad_attended = inv_rms * (
         scaled - unit_rows * jnp.mean(scaled * unit_rows, axis=-1, keepdims=True)

time: 172 us -> 161 us (0.936); the launches traced: 171 us -> 158 us
  waiting for transfers between devices: 41.2 us -> 35 us
  blocking collectives: 33.1 us -> 27 us
    psum x1 -> x0, blocking collectives: 33.1 us -> none  [on_device(): gain_grad = lax.psum(gain_part, ('seq', 'dp')) / math.sqrt(total_tokens)]
    all_gather x0 -> x1, blocking collectives: none -> 27 us  [on_device(): lax.all_gather(gain_part, ('seq', 'dp'))]
    ppermute x16, waiting for transfers between devices: 41.2 us -> 35 us  [shifted(): return lax.ppermute(block, axis, route)]
  transfers between devices with their start and end apart: 18 -> 18, of which waited for: 9 -> 9; matrix products, arithmetic and copies ran while one was open for 8% -> 9% of each run, Pallas kernels for 0% -> 0%
where the time goes in v1:
time: 161 us; the launch traced here: 158 us
  starting transfers between devices  49.1 us (30%)
  waiting for transfers between devices  35 us (22%)
  blocking collectives  27 us (17%)
  between operations  26.5 us (16%)
  matrix products  11.3 us (7%)
  local copies, waits for them, and re-layouts  5.63 us (3%)
  other arithmetic  3.3 us (2%)
    ppermute x16, starting transfers between devices, shifted(): return lax.ppermute(block, axis, route)  45.6 us
    ppermute x16, waiting for transfers between devices, shifted(): return lax.ppermute(block, axis, route)  35 us
    all_gather x1, blocking collectives, on_device(): lax.all_gather(gain_part, ('seq', 'dp'))  27 us
    dot_general x1, matrix products, on_device(): jnp.dot(exchanged, lax.all_gather(w_out, 'head', axis=0, tiled=True), pre...  3.73 us
    all_to_all x1, starting transfers between devices, on_device(): lax.all_to_all(normed_rows, 'head', split_axis=0, concat_axis=1, tiled=True)  3.44 us
  transfers between devices with their start and end apart: 18, of which 9 were waited for; matrix products, arithmetic and copies ran while one was open for 9% of the time, Pallas kernels for 0%

profile of v1, /device:TPU:7, one launch (start us, length us, event | category | flops | bytes accessed | tf_op | source)
XLA Modules:
  0.0 157.8 jit_solution(15284808434193462145)
XLA Ops:
  8.0 1.0 reshape.195
  9.2 1.0 reshape.196
  10.5 3.2 %collective-permute-start.4 = (f32[4,128,128]{2,1,0:T(8,128)S(1)}, f32[4,128,128]{2,1,0:T(8,128)S(1)}, u32[]{:S(2)}, u32[]{:S(2)}) collective-permute-start(f32[4,128,128]{2,1,0:T(8,128)S(1)} %get-tuple-element.24), channel_id=1, source_target_pairs={{0,4},{4,8},{8,12},{12,16},{16,20},{20,24},{24,28},{1,5},{5,9},{9,... | collective-permute-start | bytes 786440 | tf_op jit(solution)/shard_map/ppermute | solution.py:14
  13.6 5.9 %collective-permute-done.4 = f32[4,128,128]{2,1,0:T(8,128)S(1)} collective-permute-done((f32[4,128,128]{2,1,0:T(8,128)S(1)}, f32[4,128,128]{2,1,0:T(8,128)S(1)}, u32[]{:S(2)}, u32[]{:S(2)}) %collective-permute-start.4) | collective-permute-done | bytes 262176 | tf_op jit(solution)/shard_map/ppermute | solution.py:14
  19.5 4.0 %collective-permute-start.5 = (f32[4,128,128]{2,1,0:T(8,128)S(1)}, f32[4,128,128]{2,1,0:T(8,128)S(1)}, u32[]{:S(2)}, u32[]{:S(2)}) collective-permute-start(f32[4,128,128]{2,1,0:T(8,128)S(1)} %collective-permute-done.4), channel_id=1, source_target_pairs={{0,4},{4,8},{8,12},{12,16},{16,20},{20,24},{24,28},{1,5},{5,9},{9,... | collective-permute-start | bytes 786440 | tf_op jit(solution)/shard_map/ppermute | solution.py:14
  23.6 4.1 %collective-permute-start = (f32[1]{0:T(128)}, f32[1]{0:T(128)}, u32[]{:S(2)}, u32[]{:S(2)}) collective-permute-start(f32[1]{0:T(128)} %bitcast.1), channel_id=1, source_target_pairs={{0,4},{4,8},{8,12},{12,16},{16,20},{20,24},{24,28},{1,5},{5,9},{9,... | collective-permute-start | bytes 20 | tf_op jit(solution)/shard_map/ppermute | solution.py:14
  28.2 4.4 %collective-permute-start.1 = (f32[1]{0:T(128)}, f32[1]{0:T(128)}, u32[]{:S(2)}, u32[]{:S(2)}) collective-permute-start(f32[1]{0:T(128)} %collective-permute-done), channel_id=1, source_target_pairs={{0,4},{4,8},{8,12},{12,16},{16,20},{20,24},{24,28},{1,5},{5,9},{9,... | collective-permute-start | bytes 20 | tf_op jit(solution)/shard_map/ppermute | solution.py:14
  34.8 3.2 %collective-permute-start.6 = (f32[4,128,128]{2,1,0:T(8,128)S(1)}, f32[4,128,128]{2,1,0:T(8,128)S(1)}, u32[]{:S(2)}, u32[]{:S(2)}) collective-permute-start(f32[4,128,128]{2,1,0:T(8,128)S(1)} %fusion.14), channel_id=1, source_target_pairs={{0,8},{4,12},{8,16},{12,20},{16,24},{20,28},{1,9},{5,13},{9,17},{1... | collective-permute-start | bytes 786440 | tf_op jit(solution)/shard_map/ppermute | solution.py:14
  38.1 2.7 %fusion.7 = f32[256,512]{0,1:T(8,128)S(1)} fusion(bf16[512,2048]{1,0:T(8,128)(2,1)} %param.12, bf16[1,256,2048]{2,1,0:T(8,128)(2,1)S(1)} %copy-done), kind=kOutput, calls=%fused_computation.17 | convolution fusion | flops 536870912 | bytes 3670016 | tf_op jit(solution)/shard_map/tm,fm->tf/dot_general | solution.py:92
  42.0 3.9 %collective-permute-start.2 = (f32[1]{0:T(128)}, f32[1]{0:T(128)}, u32[]{:S(2)}, u32[]{:S(2)}) collective-permute-start(f32[1]{0:T(128)} %select_n.117), channel_id=1, source_target_pairs={{0,8},{4,12},{8,16},{12,20},{16,24},{20,28},{1,9},{5,13},{9,17},{1... | collective-permute-start | bytes 20 | tf_op jit(solution)/shard_map/ppermute | solution.py:14
  46.6 4.2 %collective-permute-start.7 = (f32[4,128,128]{2,1,0:T(8,128)S(1)}, f32[4,128,128]{2,1,0:T(8,128)S(1)}, u32[]{:S(2)}, u32[]{:S(2)}) collective-permute-start(f32[4,128,128]{2,1,0:T(8,128)S(1)} %fusion.13), channel_id=1, source_target_pairs={{0,16},{4,20},{8,24},{12,28},{1,17},{5,21},{9,25},{13,29},{2,18},{... | collective-permute-start | bytes 786440 | tf_op jit(solution)/shard_map/ppermute | solution.py:14
  52.1 2.1 %collective-permute-start.3 = (f32[1]{0:T(128)}, f32[1]{0:T(128)}, u32[]{:S(2)}, u32[]{:S(2)}) collective-permute-start(f32[1]{0:T(128)} %select_n.118), channel_id=1, source_target_pairs={{0,16},{4,20},{8,24},{12,28},{1,17},{5,21},{9,25},{13,29},{2,18},{... | collective-permute-start | bytes 20 | tf_op jit(solution)/shard_map/ppermute | solution.py:14
  56.7 4.2 %collective-permute-start.12 = (f32[4,128,128]{1,2,0:T(8,128)S(1)}, f32[4,128,128]{1,2,0:T(8,128)}, u32[]{:S(2)}, u32[]{:S(2)}) collective-permute-start(f32[4,128,128]{1,2,0:T(8,128)S(1)} %multiply_bitcast_fusion), channel_id=1, source_target_pairs={{4,0},{8,4},{12,8},{16,12},{20,16},{24,20},{28,24},{5,1},{9,5},{13... | collective-permute-start | bytes 786440 | tf_op jit(solution)/shard_map/ppermute | solution.py:14
  60.9 3.3 %collective-permute-start.8 = (f32[1]{0:T(128)}, f32[1]{0:T(128)}, u32[]{:S(2)}, u32[]{:S(2)}) collective-permute-start(f32[1]{0:T(128)} %bitcast.1), channel_id=1, source_target_pairs={{4,0},{8,4},{12,8},{16,12},{20,16},{24,20},{28,24},{5,1},{9,5},{13... | collective-permute-start | bytes 20 | tf_op jit(solution)/shard_map/ppermute | solution.py:14
  64.2 7.4 %collective-permute-done.8 = f32[1]{0:T(128)} collective-permute-done((f32[1]{0:T(128)}, f32[1]{0:T(128)}, u32[]{:S(2)}, u32[]{:S(2)}) %collective-permute-start.8) | collective-permute-done | bytes 36 | tf_op jit(solution)/shard_map/ppermute | solution.py:14
  71.6 1.9 %collective-permute-start.9 = (f32[1]{0:T(128)}, f32[1]{0:T(128)}, u32[]{:S(2)}, u32[]{:S(2)}) collective-permute-start(f32[1]{0:T(128)} %collective-permute-done.8), channel_id=1, source_target_pairs={{4,0},{8,4},{12,8},{16,12},{20,16},{24,20},{28,24},{5,1},{9,5},{13... | collective-permute-start | bytes 20 | tf_op jit(solution)/shard_map/ppermute | solution.py:14
  74.1 2.8 %collective-permute-done.9 = f32[1]{0:T(128)} collective-permute-done((f32[1]{0:T(128)}, f32[1]{0:T(128)}, u32[]{:S(2)}, u32[]{:S(2)}) %collective-permute-start.9) | collective-permute-done | bytes 36 | tf_op jit(solution)/shard_map/ppermute | solution.py:14
  78.1 1.3 collective-permute-start.10
  80.7 2.2 %collective-permute-done.10 = f32[1]{0:T(128)} collective-permute-done((f32[1]{0:T(128)}, f32[1]{0:T(128)}, u32[]{:S(2)}, u32[]{:S(2)}) %collective-permute-start.10) | collective-permute-done | bytes 36 | tf_op jit(solution)/shard_map/ppermute | solution.py:14
  83.5 1.3 collective-permute-start.11
  85.4 3.7 %collective-permute-done.11 = f32[1]{0:T(128)} collective-permute-done((f32[1]{0:T(128)}, f32[1]{0:T(128)}, u32[]{:S(2)}, u32[]{:S(2)}) %collective-permute-start.11) | collective-permute-done | bytes 36 | tf_op jit(solution)/shard_map/ppermute | solution.py:14
  90.8 1.9 %collective-permute-start.13 = (f32[4,128,128]{1,2,0:T(8,128)}, f32[4,128,128]{1,2,0:T(8,128)}, u32[]{:S(2)}, u32[]{:S(2)}) collective-permute-start(f32[4,128,128]{1,2,0:T(8,128)} %collective-permute-done.12), channel_id=1, source_target_pairs={{4,0},{8,4},{12,8},{16,12},{20,16},{24,20},{28,24},{5,1},{9,5},{13... | collective-permute-start | bytes 786440 | tf_op jit(solution)/shard_map/ppermute | solution.py:14
  93.4 0.8 copy.71
  95.1 3.4 %all-to-all-start = ((bf16[2,128,512]{1,2,0:T(8,128)(2,1)}), bf16[2,128,512]{1,2,0:T(8,128)(2,1)S(1)}, u32[]{:S(2)}, u32[]{:S(2)}) async-start(bf16[2,128,512]{1,2,0:T(8,128)(2,1)} %copy.60), calls=%async_computation | async-start | bytes 524288 | tf_op jit(solution)/shard_map/all_to_all | solution.py:85
  99.1 1.1 fusion.11
  100.2 1.3 collective-permute-start.14
  101.5 27.0 %all-gather.1 = f32[16,4,128]{2,1,0:T(4,128)S(1)} all-gather(f32[1,4,128]{2,1,0:T(4,128)S(1)} %bitcast.84), channel_id=2, replica_groups=mesh['seq'=8,'head'=2,'dp'=2] {'seq','dp'}, dimensions={0}, use_global_device_ids=true | all-gather | bytes 34816 | tf_op jit(solution)/shard_map/all_gather | solution.py:97
  128.7 1.0 fusion.10
  129.7 1.3 collective-permute-start.15
  131.6 1.3 convolution_bitcast_fusion
  132.9 11.7 %collective-permute-done.15 = f32[4,128,128]{1,2,0:T(8,128)S(1)} collective-permute-done((f32[4,128,128]{1,2,0:T(8,128)S(1)}, f32[4,128,128]{1,2,0:T(8,128)S(1)}, u32[]{:S(2)}, u32[]{:S(2)}) %collective-permute-start.15) | collective-permute-done | bytes 262176 | tf_op jit(solution)/shard_map/ppermute | solution.py:14
  147.2 3.7 %fusion = bf16[1,128,2048]{2,1,0:T(8,128)(2,1)} fusion(bf16[128,1024]{0,1:T(8,128)(2,1)S(1)} %bitcast.80, bf16[1024,2048]{1,0:T(8,128)(2,1)} %all-gather.4.cloned.1.call-done), kind=kOutput, calls=%fused_computation.1 | convolution fusion | flops 537133056 | bytes 4980736 | tf_op jit(solution)/shard_map/dot_general | solution.py:86
  (51 shorter events, 8.9 us)
Async XLA Ops:
  7.2 30.9 %copy-start = (bf16[1,256,2048]{2,1,0:T(8,128)(2,1)S(1)}, bf16[1,256,2048]{2,1,0:T(8,128)(2,1)}, u32[]{:S(2)}) copy-start(bf16[1,256,2048]{2,1,0:T(8,128)(2,1)} %param.13) | copy-start | bytes 3145732
  7.2 20.5 %copy-start.2 = (bf16[1,256,512]{2,1,0:T(8,128)(2,1)S(1)}, bf16[1,256,512]{2,1,0:T(8,128)(2,1)}, u32[]{:S(2)}) copy-start(bf16[1,256,512]{2,1,0:T(8,128)(2,1)} %param.7) | copy-start | bytes 786436
  7.2 140.0 %all-gather.4.cloned.1.call-start = ((), (), s32[]{:S(2)}) async-start(), calls=%async_computation.1 | async-start | bytes 6291456 | tf_op jit(solution)/shard_map/all_gather | solution.py:88
  10.5 9.1 %collective-permute-start.4 = (f32[4,128,128]{2,1,0:T(8,128)S(1)}, f32[4,128,128]{2,1,0:T(8,128)S(1)}, u32[]{:S(2)}, u32[]{:S(2)}) collective-permute-start(f32[4,128,128]{2,1,0:T(8,128)S(1)} %get-tuple-element.24), channel_id=1, source_target_pairs={{0,4},{4,8},{8,12},{12,16},{16,20},{20,24},{24,28},{1,5},{5,9},{9,... | collective-permute-start | bytes 786440 | tf_op jit(solution)/shard_map/ppermute | solution.py:14
  19.5 15.3 %collective-permute-start.5 = (f32[4,128,128]{2,1,0:T(8,128)S(1)}, f32[4,128,128]{2,1,0:T(8,128)S(1)}, u32[]{:S(2)}, u32[]{:S(2)}) collective-permute-start(f32[4,128,128]{2,1,0:T(8,128)S(1)} %collective-permute-done.4), channel_id=1, source_target_pairs={{0,4},{4,8},{8,12},{12,16},{16,20},{20,24},{24,28},{1,5},{5,9},{9,... | collective-permute-start | bytes 786440 | tf_op jit(solution)/shard_map/ppermute | solution.py:14
  23.6 4.6 %collective-permute-start = (f32[1]{0:T(128)}, f32[1]{0:T(128)}, u32[]{:S(2)}, u32[]{:S(2)}) collective-permute-start(f32[1]{0:T(128)} %bitcast.1), channel_id=1, source_target_pairs={{0,4},{4,8},{8,12},{12,16},{16,20},{20,24},{24,28},{1,5},{5,9},{9,... | collective-permute-start | bytes 20 | tf_op jit(solution)/shard_map/ppermute | solution.py:14
  28.2 5.3 %collective-permute-start.1 = (f32[1]{0:T(128)}, f32[1]{0:T(128)}, u32[]{:S(2)}, u32[]{:S(2)}) collective-permute-start(f32[1]{0:T(128)} %collective-permute-done), channel_id=1, source_target_pairs={{0,4},{4,8},{8,12},{12,16},{16,20},{20,24},{24,28},{1,5},{5,9},{9,... | collective-permute-start | bytes 20 | tf_op jit(solution)/shard_map/ppermute | solution.py:14
  34.8 21.2 %copy-start.3 = (f32[4,128]{1,0:T(4,128)S(1)}, f32[4,128]{1,0:T(4,128)}, u32[]{:S(2)}) copy-start(f32[4,128]{1,0:T(4,128)} %param.11) | copy-start | bytes 6148
  34.8 11.7 %collective-permute-start.6 = (f32[4,128,128]{2,1,0:T(8,128)S(1)}, f32[4,128,128]{2,1,0:T(8,128)S(1)}, u32[]{:S(2)}, u32[]{:S(2)}) collective-permute-start(f32[4,128,128]{2,1,0:T(8,128)S(1)} %fusion.14), channel_id=1, source_target_pairs={{0,8},{4,12},{8,16},{12,20},{16,24},{20,28},{1,9},{5,13},{9,17},{1... | collective-permute-start | bytes 786440 | tf_op jit(solution)/shard_map/ppermute | solution.py:14
  42.0 3.9 %collective-permute-start.2 = (f32[1]{0:T(128)}, f32[1]{0:T(128)}, u32[]{:S(2)}, u32[]{:S(2)}) collective-permute-start(f32[1]{0:T(128)} %select_n.117), channel_id=1, source_target_pairs={{0,8},{4,12},{8,16},{12,20},{16,24},{20,28},{1,9},{5,13},{9,17},{1... | collective-permute-start | bytes 20 | tf_op jit(solution)/shard_map/ppermute | solution.py:14
  46.6 8.8 %collective-permute-start.7 = (f32[4,128,128]{2,1,0:T(8,128)S(1)}, f32[4,128,128]{2,1,0:T(8,128)S(1)}, u32[]{:S(2)}, u32[]{:S(2)}) collective-permute-start(f32[4,128,128]{2,1,0:T(8,128)S(1)} %fusion.13), channel_id=1, source_target_pairs={{0,16},{4,20},{8,24},{12,28},{1,17},{5,21},{9,25},{13,29},{2,18},{... | collective-permute-start | bytes 786440 | tf_op jit(solution)/shard_map/ppermute | solution.py:14
  52.1 2.1 %collective-permute-start.3 = (f32[1]{0:T(128)}, f32[1]{0:T(128)}, u32[]{:S(2)}, u32[]{:S(2)}) collective-permute-start(f32[1]{0:T(128)} %select_n.118), channel_id=1, source_target_pairs={{0,16},{4,20},{8,24},{12,28},{1,17},{5,21},{9,25},{13,29},{2,18},{... | collective-permute-start | bytes 20 | tf_op jit(solution)/shard_map/ppermute | solution.py:14
  56.7 34.1 %collective-permute-start.12 = (f32[4,128,128]{1,2,0:T(8,128)S(1)}, f32[4,128,128]{1,2,0:T(8,128)}, u32[]{:S(2)}, u32[]{:S(2)}) collective-permute-start(f32[4,128,128]{1,2,0:T(8,128)S(1)} %multiply_bitcast_fusion), channel_id=1, source_target_pairs={{4,0},{8,4},{12,8},{16,12},{20,16},{24,20},{28,24},{5,1},{9,5},{13... | collective-permute-start | bytes 786440 | tf_op jit(solution)/shard_map/ppermute | solution.py:14
  60.9 10.7 %collective-permute-start.8 = (f32[1]{0:T(128)}, f32[1]{0:T(128)}, u32[]{:S(2)}, u32[]{:S(2)}) collective-permute-start(f32[1]{0:T(128)} %bitcast.1), channel_id=1, source_target_pairs={{4,0},{8,4},{12,8},{16,12},{20,16},{24,20},{28,24},{5,1},{9,5},{13... | collective-permute-start | bytes 20 | tf_op jit(solution)/shard_map/ppermute | solution.py:14
  71.6 5.3 %collective-permute-start.9 = (f32[1]{0:T(128)}, f32[1]{0:T(128)}, u32[]{:S(2)}, u32[]{:S(2)}) collective-permute-start(f32[1]{0:T(128)} %collective-permute-done.8), channel_id=1, source_target_pairs={{4,0},{8,4},{12,8},{16,12},{20,16},{24,20},{28,24},{5,1},{9,5},{13... | collective-permute-start | bytes 20 | tf_op jit(solution)/shard_map/ppermute | solution.py:14
  78.1 4.8 %collective-permute-start.10 = (f32[1]{0:T(128)}, f32[1]{0:T(128)}, u32[]{:S(2)}, u32[]{:S(2)}) collective-permute-start(f32[1]{0:T(128)} %select_n.135), channel_id=1, source_target_pairs={{8,0},{12,4},{16,8},{20,12},{24,16},{28,20},{9,1},{13,5},{17,9},{2... | collective-permute-start | bytes 20 | tf_op jit(solution)/shard_map/ppermute | solution.py:14
  83.5 5.6 %collective-permute-start.11 = (f32[1]{0:T(128)}, f32[1]{0:T(128)}, u32[]{:S(2)}, u32[]{:S(2)}) collective-permute-start(f32[1]{0:T(128)} %select_n.136), channel_id=1, source_target_pairs={{16,0},{20,4},{24,8},{28,12},{17,1},{21,5},{25,9},{29,13},{18,2},{... | collective-permute-start | bytes 20 | tf_op jit(solution)/shard_map/ppermute | solution.py:14
  90.8 2.6 %copy-start.1 = (bf16[4,256,256]{2,1,0:T(8,128)(2,1)}, bf16[4,256,256]{2,1,0:T(8,128)(2,1)S(1)}, u32[]{:S(2)}) copy-start(bf16[4,256,256]{2,1,0:T(8,128)(2,1)S(1)} %fusion.2) | copy-start | bytes 1572868
  90.8 8.3 %collective-permute-start.13 = (f32[4,128,128]{1,2,0:T(8,128)}, f32[4,128,128]{1,2,0:T(8,128)}, u32[]{:S(2)}, u32[]{:S(2)}) collective-permute-start(f32[4,128,128]{1,2,0:T(8,128)} %collective-permute-done.12), channel_id=1, source_target_pairs={{4,0},{8,4},{12,8},{16,12},{20,16},{24,20},{28,24},{5,1},{9,5},{13... | collective-permute-start | bytes 786440 | tf_op jit(solution)/shard_map/ppermute | solution.py:14
  95.1 52.1 %all-to-all-start = ((bf16[2,128,512]{1,2,0:T(8,128)(2,1)}), bf16[2,128,512]{1,2,0:T(8,128)(2,1)S(1)}, u32[]{:S(2)}, u32[]{:S(2)}) async-start(bf16[2,128,512]{1,2,0:T(8,128)(2,1)} %copy.60), calls=%async_computation | async-start | bytes 524288 | tf_op jit(solution)/shard_map/all_to_all | solution.py:85
  100.2 28.5 %collective-permute-start.14 = (f32[4,128,128]{1,2,0:T(8,128)S(1)}, f32[4,128,128]{1,2,0:T(8,128)}, u32[]{:S(2)}, u32[]{:S(2)}) collective-permute-start(f32[4,128,128]{1,2,0:T(8,128)S(1)} %fusion.11), channel_id=1, source_target_pairs={{8,0},{12,4},{16,8},{20,12},{24,16},{28,20},{9,1},{13,5},{17,9},{2... | collective-permute-start | bytes 786440 | tf_op jit(solution)/shard_map/ppermute | solution.py:14
  129.7 14.9 %collective-permute-start.15 = (f32[4,128,128]{1,2,0:T(8,128)S(1)}, f32[4,128,128]{1,2,0:T(8,128)S(1)}, u32[]{:S(2)}, u32[]{:S(2)}) collective-permute-start(f32[4,128,128]{1,2,0:T(8,128)S(1)} %fusion.10), channel_id=1, source_target_pairs={{16,0},{20,4},{24,8},{28,12},{17,1},{21,5},{25,9},{29,13},{18,2},{... | collective-permute-start | bytes 786440 | tf_op jit(solution)/shard_map/ppermute | solution.py:14
Sparse Core Ops, SparseCore 0:
  27.8 57.8 all-gather.3
